TPU v7x, 128 devices: a whole 4x4x4 slice. The times are simulated.
128 devices in a mesh: row: 8 (over y, core), col: 16 (over z, x).
Axes of the slice: x: 4, y: 4, z: 4, core: 2. Of those that a mesh axis runs over, the one named last changes fastest.
Arguments:
- kernel_panel: float32 [64, 32768], P(None, ('row', 'col')), may hold values from -4 to 16, as said below
- kernel_slab: float32 [32768, 4096], P('row', 'col'), may hold values from -4 to 20, as said below
- targets: float32 [256, 32768], P(None, ('row', 'col')), may hold values from -6 to 6
Outputs:
- updated_slab: float32 [32768, 4096], P('row', 'col')
- solved_targets: float32 [256, 32768], P('col', 'row')
- panel_factor: float32 [64, 32768], P(None, ('row', 'col'))
Inputs may be any that keep to these rules, and one draw needn't show every extreme that they name: kernel_panel[:, 0:64] is symmetric and positive definite. `kernel_slab`: rows 0 to 63 equal kernel_panel[:, 32768 - 4096 : 32768]; the last 4096 rows form a symmetric matrix.
All inputs are finite; a program needn't handle non-finite values.
Results may differ from a plain program's by a relative error of at most 0.00018.
Values sent between devices are 32-bit elements; how exact they have to be, the bound alone decides.
No kernel may reach another device: no remote copies, remote signals or barrier semaphores. Data moves between devices by JAX's collectives and lax.ppermute only.
A program may use at most 64 MiB of HBM per device.

v0:
```python
import jax
import jax.numpy as jnp
from jax import lax
from jax.sharding import PartitionSpec as P


def spread(block, axis, source):
    block = jnp.where(lax.axis_index(axis) == source, block, jnp.zeros_like(block))
    return lax.psum(block, axis)


def lower_solve(factor, values):
    return jax.scipy.linalg.solve_triangular(factor, values, lower=True)


def body(kernel_panel, kernel_slab, targets):
    highest = lax.Precision.HIGHEST
    panel_width = kernel_panel.shape[0]
    row_count = lax.axis_size("row")
    row_index = lax.axis_index("row")
    flat_index = lax.axis_index(("row", "col"))
    corner_rows = jnp.concatenate([kernel_panel[:, :panel_width], targets[:, :panel_width]], 0)
    shared = spread(corner_rows, ("row", "col"), 0)
    lower_factor = jnp.linalg.cholesky(shared[:panel_width])
    panel_factor = lower_solve(lower_factor, kernel_panel)
    gathered = lax.all_gather(panel_factor, "col", axis=1, tiled=True)
    slab_factor = spread(panel_factor, "row", row_count - 1)
    product = lax.dot_general(
        gathered,
        slab_factor,
        (((0,), (0,)), ((), ())),
        precision=highest,
        preferred_element_type=jnp.float32,
    )
    update = kernel_slab - product
    head_rows = jnp.where(row_index == 0, slab_factor, update[:panel_width])
    updated_slab = jnp.concatenate([head_rows, update[panel_width:]], 0)
    solved_lead = lower_solve(lower_factor, shared[panel_width:].T).T
    result = targets - jnp.dot(
        solved_lead, panel_factor, precision=highest, preferred_element_type=jnp.float32
    )
    head_cols = jnp.where(flat_index == 0, solved_lead, result[:, :panel_width])
    result = jnp.concatenate([head_cols, result[:, panel_width:]], 1)
    solved_targets = lax.all_to_all(result, "col", split_axis=0, concat_axis=1, tiled=True)
    return (updated_slab, solved_targets, panel_factor)


def solution(mesh):
    in_specs = (P(None, ("row", "col")), P("row", "col"), P(None, ("row", "col")))
    out_specs = (P("row", "col"), P("col", "row"), P(None, ("row", "col")))
    return jax.shard_map(body, mesh=mesh, in_specs=in_specs, out_specs=out_specs, check_vma=False)
```

profile of v0, /device:TPU:0, one launch (start us, length us, event | category | flops | bytes accessed | tf_op | source)
XLA Modules:
  0.0 286.8 jit_solution(15664791899250229156)
XLA Ops:
  7.2 0.8 slice.34
  8.1 1.1 copy.17
  9.2 0.7 maximum_select_fusion
  10.0 143.3 %all-reduce.3.cloned.1.call-done = f32[320,64]{0,1:T(8,128)} async-done(((f32[320,64]{0,1:T(8,128)}), f32[320,64]{0,1:T(8,128)}) %all-reduce.3.cloned.1.call-update) | async-done | bytes 81936 | tf_op jit(solution)/shard_map/psum | solution.py:9
  153.3 0.8 slice.43
  154.1 0.8 fusion.5
  154.9 5.8 %cholesky.18 = f32[64,64]{1,0:T(8,128)S(1)} custom-call(f32[64,64]{1,0:T(8,128)S(1)} %fusion.5), custom_call_target="Cholesky" | custom-call | tf_op jit(solution)/shard_map/jit(cholesky)/cholesky | solution.py:24
  160.8 0.6 compare_reduce_fusion
  161.4 0.7 fusion.1
  162.1 4.9 %custom-call.7 = f32[1,64,64]{1,2,0:T(8,128)S(1)} custom-call(f32[1,64,64]{2,1,0:T(8,128)S(1)} %fusion.1), custom_call_target="InvertDiagBlocksLowerTriangular" | custom-call | tf_op jit(solution)/shard_map/jit(_solve_triangular)/triangular_solve | solution.py:13
  167.0 1.8 broadcast_select_fusion
  168.8 0.7 all-gather.2.cloned.1.call-update
  169.5 1.2 fusion
  170.7 1.3 convolution_subtract_fusion.1
  172.0 0.8 copy.20
  172.9 5.6 %all-to-all-start = ((f32[16,16,256]{2,1,0:T(8,128)}), f32[16,16,256]{2,1,0:T(8,128)S(1)}, u32[]{:S(2)}, u32[]{:S(2)}) async-start(f32[16,16,256]{2,1,0:T(8,128)} %bitcast.7), calls=%async_computation | async-start | bytes 524288 | tf_op jit(solution)/shard_map/all_to_all | solution.py:44
  178.5 8.7 %all-to-all-done = f32[16,16,256]{2,1,0:T(8,128)S(1)} async-done(((f32[16,16,256]{2,1,0:T(8,128)}), f32[16,16,256]{2,1,0:T(8,128)S(1)}, u32[]{:S(2)}, u32[]{:S(2)}) %all-to-all-start) | async-done | bytes 262176 | tf_op jit(solution)/shard_map/all_to_all | solution.py:44
  187.2 0.7 copy.23
  187.9 38.0 %all-reduce.5.cloned.1.call-done = f32[64,256]{1,0:T(8,128)} async-done(((f32[64,256]{1,0:T(8,128)}), f32[64,256]{1,0:T(8,128)}) %all-reduce.5.cloned.1.call-update) | async-done | bytes 65552 | tf_op jit(solution)/shard_map/psum | solution.py:9
  225.9 45.2 %all-gather.2.cloned.1.call-done = f32[64,4096]{1,0:T(8,128)} async-done(((f32[64,256]{1,0:T(8,128)}), f32[64,4096]{1,0:T(8,128)}) %all-gather.2.cloned.1.call-update) | async-done | bytes 1048592 | tf_op jit(solution)/shard_map/all_gather | solution.py:26
  271.1 6.0 %convolution_subtract_fusion = f32[4096,256]{1,0:T(8,128)S(1)} fusion(f32[4096,256]{1,0:T(8,128)} %param.6, f32[64,4096]{1,0:T(8,128)} %all-gather.2.cloned.1.call-done, f32[64,256]{1,0:T(8,128)} %all-reduce.5.cloned.1.call-done), kind=kOutput, calls=%fused_computation | convolution fusion | flops 806354944 | bytes 9502720 | tf_op jit(solution)/shard_map/dot_general | solution.py:28
  277.1 0.3 slice.45
  277.4 0.6 copy-done
  278.0 2.3 pad_maximum_fusion
  (14 shorter events, 0.4 us)
Async XLA Ops:
  7.2 146.1 %all-reduce.3.cloned.1.call-start = ((), (), s32[]{:S(2)}) async-start(), calls=%async_computation.1 | async-start | bytes 196608 | tf_op jit(solution)/shard_map/psum | solution.py:9
  9.9 216.0 %all-reduce.5.cloned.1.call-start = ((), (), s32[]{:S(2)}) async-start(), calls=%async_computation.2 | async-start | bytes 131072 | tf_op jit(solution)/shard_map/psum | solution.py:9
  168.8 102.3 %all-gather.2.cloned.1.call-start = ((), (), s32[]{:S(2)}) async-start(), calls=%async_computation.3 | async-start | bytes 1114112 | tf_op jit(solution)/shard_map/all_gather | solution.py:26
  172.9 14.3 %all-to-all-start = ((f32[16,16,256]{2,1,0:T(8,128)}), f32[16,16,256]{2,1,0:T(8,128)S(1)}, u32[]{:S(2)}, u32[]{:S(2)}) async-start(f32[16,16,256]{2,1,0:T(8,128)} %bitcast.7), calls=%async_computation | async-start | bytes 524288 | tf_op jit(solution)/shard_map/all_to_all | solution.py:44
  277.1 0.8 copy-start
Sparse Core Ops, SparseCore 0:
  13.3 139.9 all-reduce.2
  168.9 56.9 all-reduce.4
  228.6 42.4 all-gather.1
where the time goes:
time: 287 us
  waiting for transfers between devices  236 us (82%)
  other arithmetic  15.9 us (6%)
  between operations  13.9 us (5%)
  matrix products  10.2 us (4%)
  starting transfers between devices  5.75 us (2%)
  local copies, waits for them, and re-layouts  5.16 us (2%)
    psum x2, waiting for transfers between devices, spread(): return lax.psum(block, axis)  181 us
    all_gather x1, waiting for transfers between devices, body(): gathered = lax.all_gather(panel_factor, 'col', axis=1, tiled=True)  45.2 us
    all_to_all x1, waiting for transfers between devices, body(): lax.all_to_all(result, 'col', split_axis=0, concat_axis=1, tiled=True)  8.69 us
    another operation x3, other arithmetic, body(): lower_factor = jnp.linalg.cholesky(shared[:panel_width])  6.52 us
    dot_general x1, matrix products, body(): lax.dot_general(gathered, slab_factor, (((0,), (0,)), ((), ())), precisio...  6 us
  transfers between devices with their start and end apart: 4, of which 4 were waited for; matrix products, arithmetic and copies ran while one was open for 1% of the time, Pallas kernels for 0%

commit v1 on v0

--- a/solution.py
+++ b/solution.py
@@ -5,8 +5,13 @@
 
 
 def spread(block, axis, source):
+
+    def begin_points(block_here, comm_axis):
+        side_arr = jnp.sum(lax.all_gather(block_here, comm_axis), axis=0)
+        return side_arr
+
     block = jnp.where(lax.axis_index(axis) == source, block, jnp.zeros_like(block))
-    return lax.psum(block, axis)
+    return begin_points(block, axis)
 
 
 def lower_solve(factor, values):

time: 287 us -> 165 us (0.57)
  waiting for transfers between devices: 236 us -> 98.3 us
  blocking collectives: 0 us -> 13.1 us
  other arithmetic: 15.9 us -> 20.4 us
    psum x2 -> x0, waiting for transfers between devices: 181 us -> none  [spread(): return lax.psum(block, axis)]
    all_gather x0 -> x1, waiting for transfers between devices: none -> 77.5 us  [begin_points(): side_arr = jnp.sum(lax.all_gather(block_here, comm_axis), axis=0)]
    all_gather x1, waiting for transfers between devices: 45.2 us -> 20.7 us  [body(): gathered = lax.all_gather(panel_factor, 'col', axis=1, tiled=True)]
    all_gather x0 -> x1, blocking collectives: none -> 13.1 us  [begin_points(): side_arr = jnp.sum(lax.all_gather(block_here, comm_axis), axis=0)]
    all_to_all x1, waiting for transfers between devices: 8.69 us -> 0.01 us  [body(): lax.all_to_all(result, 'col', split_axis=0, concat_axis=1, tiled=True)]
    reduce_sum x0 -> x2, other arithmetic: none -> 5.3 us  [begin_points(): side_arr = jnp.sum(lax.all_gather(block_here, comm_axis), axis=0)]
  transfers between devices with their start and end apart: 4 -> 3, of which waited for: 4 -> 2; matrix products, arithmetic and copies ran while one was open for 1% -> 2% of each run, Pallas kernels for 0% -> 0%
where the time goes in v1:
time: 165 us
  waiting for transfers between devices  98.3 us (60%)
  other arithmetic  20.4 us (12%)
  between operations  14.2 us (9%)
  blocking collectives  13.1 us (8%)
  matrix products  8.43 us (5%)
  starting transfers between devices  6.5 us (4%)
  local copies, waits for them, and re-layouts  4.03 us (2%)
    all_gather x1, waiting for transfers between devices, begin_points(): side_arr = jnp.sum(lax.all_gather(block_here, comm_axis), axis=0)  77.5 us
    all_gather x1, waiting for transfers between devices, body(): gathered = lax.all_gather(panel_factor, 'col', axis=1, tiled=True)  20.7 us
    all_gather x1, blocking collectives, begin_points(): side_arr = jnp.sum(lax.all_gather(block_here, comm_axis), axis=0)  13.1 us
    another operation x3, other arithmetic, body(): lower_factor = jnp.linalg.cholesky(shared[:panel_width])  6.52 us
    all_to_all x1, starting transfers between devices, body(): lax.all_to_all(result, 'col', split_axis=0, concat_axis=1, tiled=True)  6.42 us
    dot_general x1, matrix products, body(): lax.dot_general(gathered, slab_factor, (((0,), (0,)), ((), ())), precisio...  5.98 us
    another operation x2, other arithmetic, lower_solve(): return jax.scipy.linalg.solve_triangular(factor, values, lower=True)  5.55 us
    reduce_sum x2, other arithmetic, begin_points(): side_arr = jnp.sum(lax.all_gather(block_here, comm_axis), axis=0)  5.3 us
  transfers between devices with their start and end apart: 3, of which 2 were waited for; matrix products, arithmetic and copies ran while one was open for 2% of the time, Pallas kernels for 0%

profile of v1, /device:TPU:0, one launch (start us, length us, event | category | flops | bytes accessed | tf_op | source)
XLA Modules:
  0.0 165.0 jit_solution(8971502408998451964)
XLA Ops:
  7.2 1.1 copy.17
  8.3 0.8 slice.34
  9.1 0.1 copy.25
  9.2 0.7 maximum_select_fusion
  10.0 77.5 %all-gather.4.cloned.1.call-done = f32[128,320,64]{1,2,0:T(8,128)} async-done(((f32[1,320,64]{1,2,0:T(8,128)}), f32[128,320,64]{1,2,0:T(8,128)}) %all-gather.4.cloned.1.call-update) | async-done | bytes 10485776 | tf_op jit(solution)/shard_map/all_gather | solution.py:10
  87.5 5.3 %reduce_sum.18 = f32[320,64]{0,1:T(8,128)S(1)} reduce(f32[128,320,64]{1,2,0:T(8,128)} %all-gather.4.cloned.1.call-done, f32[]{:T(128)} %constant.56.clone.1), dimensions={0}, to_apply=%region_0.1 | reduce | flops 2600960 | bytes 10567684 | tf_op jit(solution)/shard_map/reduce_sum | solution.py:10
  92.7 0.1 copy.27
  92.8 5.8 %cholesky.18 = f32[64,64]{1,0:T(8,128)S(1)} custom-call(f32[64,64]{1,0:T(8,128)S(1)} %fusion.6), custom_call_target="Cholesky" | custom-call | tf_op jit(solution)/shard_map/jit(cholesky)/cholesky | solution.py:29
  98.7 0.6 compare_reduce_fusion
  99.4 0.7 fusion.2
  100.0 4.9 %custom-call.7 = f32[1,64,64]{1,2,0:T(8,128)S(1)} custom-call(f32[1,64,64]{2,1,0:T(8,128)S(1)} %fusion.2), custom_call_target="InvertDiagBlocksLowerTriangular" | custom-call | tf_op jit(solution)/shard_map/jit(_solve_triangular)/triangular_solve | solution.py:18
  104.9 0.9 broadcast_select_fusion
  105.8 0.1 slice.46
  105.9 0.1 copy.28
  106.0 0.3 fusion
  106.3 1.3 convolution_subtract_fusion.1
  107.7 0.8 copy.22
  108.5 6.4 %all-to-all-start = ((f32[16,16,256]{2,1,0:T(8,128)}), f32[16,16,256]{2,1,0:T(8,128)S(1)}, u32[]{:S(2)}, u32[]{:S(2)}) async-start(f32[16,16,256]{2,1,0:T(8,128)} %bitcast.10), calls=%async_computation | async-start | bytes 524288 | tf_op jit(solution)/shard_map/all_to_all | solution.py:49
  114.9 13.1 %all-gather = f32[512,256]{1,0:T(8,128)S(1)} all-gather(f32[64,256]{1,0:T(8,128)S(1)} %get-tuple-element.4), channel_id=2, replica_groups=mesh['row'=8,'col'=16] {'row'}, dimensions={0}, use_global_device_ids=true | all-gather | bytes 589824 | tf_op jit(solution)/shard_map/all_gather | solution.py:10
  128.1 0.7 copy.29
  128.8 20.7 %all-gather.6.cloned.1.call-done = f32[64,4096]{1,0:T(8,128)} async-done(((f32[64,256]{1,0:T(8,128)}), f32[64,4096]{1,0:T(8,128)}) %all-gather.6.cloned.1.call-update) | async-done | bytes 1048592 | tf_op jit(solution)/shard_map/all_gather | solution.py:31
  149.6 6.0 %convolution_subtract_fusion = f32[4096,256]{1,0:T(8,128)S(1)} fusion(f32[4096,256]{1,0:T(8,128)} %param.6, f32[64,4096]{1,0:T(8,128)} %all-gather.6.cloned.1.call-done, f32[64,256]{1,0:T(8,128)S(1)} %reduce_sum.19), kind=kOutput, calls=%fused_computation | convolution fusion | flops 806354944 | bytes 9502720 | tf_op jit(solution)/shard_map/dot_general | solution.py:33
  155.6 0.3 slice.45
  155.8 2.3 %pad_maximum_fusion = f32[4096,256]{1,0:T(8,128)} fusion(f32[4032,256]{1,0:T(8,128)S(1)} %slice.45, f32[64,256]{1,0:T(8,128)S(1)} %slice_select_fusion.1), kind=kLoop, calls=%fused_computation.1 | loop fusion | flops 1048576 | bytes 8388608 | tf_op jit(solution)/shard_map/concatenate | solution.py:42
  (16 shorter events, 0.3 us)
Async XLA Ops:
  7.2 80.3 %all-gather.4.cloned.1.call-start = ((), (), s32[]{:S(2)}) async-start(), calls=%async_computation.1 | async-start | bytes 12681216 | tf_op jit(solution)/shard_map/all_gather | solution.py:10
  9.9 139.6 %all-gather.6.cloned.1.call-start = ((), (), s32[]{:S(2)}) async-start(), calls=%async_computation.2 | async-start | bytes 1114112 | tf_op jit(solution)/shard_map/all_gather | solution.py:31
  10.0 94.9 %copy-start = (f32[64,256]{1,0:T(8,128)S(1)}, f32[64,256]{1,0:T(8,128)}, u32[]{:S(2)}) copy-start(f32[64,256]{1,0:T(8,128)} %param.5) | copy-start | bytes 196612
  108.5 19.6 %all-to-all-start = ((f32[16,16,256]{2,1,0:T(8,128)}), f32[16,16,256]{2,1,0:T(8,128)S(1)}, u32[]{:S(2)}, u32[]{:S(2)}) async-start(f32[16,16,256]{2,1,0:T(8,128)} %bitcast.10), calls=%async_computation | async-start | bytes 524288 | tf_op jit(solution)/shard_map/all_to_all | solution.py:49
Sparse Core Ops, SparseCore 0:
  11.7 75.7 all-gather.3
  106.0 43.5 all-gather.5
